TPU v7x, 32 devices: a whole 2x2x4 slice. The times are simulated.
32 devices in a mesh: feat: 4 (over y, core), rows: 8 (over z, x).
Axes of the slice: x: 2, y: 2, z: 4, core: 2. Of those that a mesh axis runs over, the one named last changes fastest.
Arguments:
- bin_index: int32 [64, 65536], P('feat', 'rows'), may hold values from 0 to 255
- node_ids: int32 [65536], P('rows'), may hold values from 0 to 7
- gradients: int32 [65536], P('rows'), may hold values from -32 to 32
- hessians: int32 [65536], P('rows'), may hold values from 1 to 32
Outputs:
- split_gains: float32 [8, 64, 256], P('rows', 'feat')
- best_gains: float32 [8], P('rows')
All inputs are finite; a program needn't handle non-finite values.
Results may differ from a plain program's by a relative error of at most 0.0003.
Values sent between devices are 32-bit elements; how exact they have to be, the bound alone decides.
No kernel may reach another device: no remote copies, remote signals or barrier semaphores. Data moves between devices by JAX's collectives and lax.ppermute only.
A program may use at most 64 MiB of HBM per device.

v0:
```python
import jax
import jax.numpy as jnp
from jax import lax
from jax.sharding import PartitionSpec as P

BINS = 256
NODE_DEV = 1


shrinkage = 1.0


def gains_of(grad_hist, hess_hist):
    left_grad = jnp.cumsum(grad_hist, axis=-1)
    left_hess = jnp.cumsum(hess_hist, axis=-1)
    total_grad = left_grad[..., -1:]
    total_hess = left_hess[..., -1:]
    right_grad = total_grad - left_grad
    right_hess = total_hess - left_hess
    return 0.5 * (
        left_grad * left_grad / (left_hess + shrinkage)
        + right_grad * right_grad / (right_hess + shrinkage)
        - total_grad * total_grad / (total_hess + shrinkage)
    )


def per_device(bin_index, node_ids, gradients, hessians):
    feature_count, rows_here = bin_index.shape
    row_block = min(4096, rows_here)
    block_count = rows_here // row_block
    paired = jnp.stack([gradients, hessians], axis=1).astype(jnp.float32)
    bin_values = jnp.arange(BINS, dtype=jnp.int32)
    every_node = NODE_DEV * lax.axis_size("rows")
    node_values = jnp.arange(every_node, dtype=jnp.int32)

    def accumulate(running, block_number):
        offset = block_number * row_block
        bins_here = lax.dynamic_slice_in_dim(bin_index, offset, row_block, 1)
        nodes_here = lax.dynamic_slice_in_dim(node_ids, offset, row_block, 0)
        values_here = lax.dynamic_slice_in_dim(paired, offset, row_block, 0)
        node_hot = (nodes_here[:, None] - 0 == node_values[None, :]).astype(jnp.float32)
        weighted = (
            (node_hot[:, :, None] * values_here[:, None, :])
            .astype(jnp.bfloat16)
            .reshape(row_block, every_node * 2)
        )
        updated = []
        for feature_index in range(feature_count):
            bin_hot = (bins_here[feature_index][:, None] == bin_values[None, :]).astype(
                jnp.bfloat16
            )
            product = lax.dot_general(
                weighted, bin_hot, (((0,), (0,)), ((), ())), preferred_element_type=jnp.float32
            )
            updated.append(running[feature_index] + product)
        return (tuple(updated), None)

    start_sums = tuple(
        (jnp.zeros((every_node * 2, BINS), jnp.float32) for feature_index in range(feature_count))
    )
    summed, unused = lax.scan(accumulate, start_sums, jnp.arange(block_count, dtype=jnp.int32))
    joined = jnp.stack(summed, axis=1)
    whole_table = joined.reshape(every_node, 2, feature_count, BINS)
    owned = lax.psum_scatter(whole_table, "rows", scatter_dimension=0, tiled=True)
    split_gains = gains_of(owned[:, 0], owned[:, 1])
    local_best = jnp.max(split_gains, axis=(1, 2))
    best_gains = lax.pmax(local_best, "feat")
    return (split_gains, best_gains)


def solution(mesh):
    in_specs = (P("feat", "rows"), P("rows"), P("rows"), P("rows"))
    out_specs = (P("rows", "feat", None), P("rows"))
    return jax.shard_map(
        per_device, mesh=mesh, in_specs=in_specs, out_specs=out_specs, check_vma=False
    )
```

profile of v0, /device:TPU:0, one launch (start us, length us, event | category | flops | bytes accessed | tf_op | source)
XLA Modules:
  0.0 124.5 jit_solution(11490770877234511038)
XLA Ops:
  7.4 0.8 add_convert_fusion
  8.2 31.2 %while.42 = (s32[]{:T(128)}, f32[16,256]{1,0:T(8,128)S(1)}, f32[16,256]{1,0:T(8,128)S(1)}, f32[16,256]{1,0:T(8,128)S(1)}, f32[16,256]{1,0:T(8,128)S(1)}, /*index...) while((s32[]{:T(128)}, f32[16,256]{1,0:T(8,128)S(1)}, ...), condition=%wide.region_1.2_spmd.clone.clone, body=%wide.region_0.1_spmd.clone.clone.sunk | while | flops 553975808 | bytes 6308552 | solution.py:61
  11.8 0.8 fusion.126
  12.6 0.8 fusion.127
  13.4 0.8 fusion.128
  14.2 0.8 fusion.129
  15.0 0.8 fusion.130
  15.8 0.8 fusion.131
  16.6 0.8 fusion.132
  17.4 0.8 fusion.133
  18.2 0.8 fusion.134
  19.0 0.8 fusion.135
  19.8 0.8 fusion.136
  20.6 0.8 fusion.137
  21.4 0.8 fusion.138
  22.2 0.8 fusion.139
  27.4 0.8 fusion.126
  29.8 0.8 fusion.129
  32.2 0.8 fusion.132
  36.2 0.8 fusion.137
  38.6 0.8 fusion.140
  39.8 1.7 %stack.79 = f32[8,2,16,256]{3,2,1,0:T(8,128)} concatenate(f32[8,2,1,256]{3,2,1,0:T(1,128)S(1)} %stack.63, f32[8,2,1,256]{3,2,1,0:T(1,128)S(1)} %stack.64, f32[8,2,1,256]{3,2,1,0:T(1,128)S(1)} %stack.65, f32[8,2,1,256]{3,2,1,0:T(1,128)S(1)} %stack.66, f32[8,2,1,256]{3,2,1,0:T(1,128)S(1)} %stack.67, f32[8,2,1,256]{3,2,1,0:T(1,128)S(1)} %stack.68, f32[8,2,1,256]{3,2,1,0:T(1,128)S(1)} %stack.69, ...), dimensions={2} | concatenate | bytes 524288 | tf_op jit(solution)/shard_map/stack | solution.py:62
  41.6 65.3 %reduce-scatter.2.cloned.1.call-done = f32[1,2,16,256]{3,2,1,0:T(8,128)} async-done(((f32[8,2,16,256]{3,2,1,0:T(8,128)}), f32[1,2,16,256]{3,2,1,0:T(8,128)}) %reduce-scatter.2.cloned.1.call-update) | async-done | bytes 32784 | tf_op jit(solution)/shard_map/reduce_scatter | solution.py:64
  110.8 6.3 %pmax.7 = f32[1]{0:T(128)} all-reduce(f32[1]{0:T(128)} %bitcast.8), channel_id=1, replica_groups=mesh['feat'=4,'rows'=8] {'feat'}, use_global_device_ids=true, to_apply=%region_8.9 | all-reduce | flops 1 | bytes 8 | tf_op jit(solution)/shard_map/pmax | solution.py:67
  (90 shorter events, 19.5 us)
Async XLA Ops:
  7.2 99.7 %reduce-scatter.2.cloned.1.call-start = ((), (), s32[]{:S(2)}) async-start(), calls=%async_computation.1 | async-start | bytes 294912 | tf_op jit(solution)/shard_map/reduce_scatter | solution.py:64
  8.2 2.2 %copy-start = (s32[16,8192]{1,0:T(8,128)S(1)}, s32[16,8192]{1,0:T(8,128)}, u32[]{:S(2)}) copy-start(s32[16,8192]{1,0:T(8,128)} %get-tuple-element.657) | copy-start | bytes 1572868 | tf_op jit(solution)/shard_map/while
  23.8 2.2 %copy-start = (s32[16,8192]{1,0:T(8,128)S(1)}, s32[16,8192]{1,0:T(8,128)}, u32[]{:S(2)}) copy-start(s32[16,8192]{1,0:T(8,128)} %get-tuple-element.657) | copy-start | bytes 1572868 | tf_op jit(solution)/shard_map/while
Sparse Core Ops, SparseCore 0:
  41.7 65.1 reduce-scatter.1
where the time goes:
time: 125 us
  waiting for transfers between devices  65.3 us (52%)
  matrix products  25.6 us (20%)
  between operations  14.3 us (11%)
  local copies, waits for them, and re-layouts  8.03 us (6%)
  blocking collectives  6.27 us (5%)
  other arithmetic  3.53 us (3%)
  loops' own time  1.41 us (1%)
    reduce_scatter x1, waiting for transfers between devices, per_device(): lax.psum_scatter(whole_table, 'rows', scatter_dimension=0, tiled=True)  65.3 us
    dot_general x32, matrix products, accumulate(): lax.dot_general(weighted, bin_hot, (((0,), (0,)), ((), ())), preferred_el...  25.6 us
    pmax x1, blocking collectives, per_device(): best_gains = lax.pmax(local_best, 'feat')  6.27 us
  transfers between devices with their start and end apart: 1, of which 1 were waited for; matrix products, arithmetic and copies ran while one was open for 0% of the time, Pallas kernels for 0%

commit v1 on v0

v1 whole, which is shorter than its diff:
```python
import functools

import jax
import jax.numpy as jnp
from jax import lax
from jax.experimental import pallas as pl
from jax.experimental.pallas import tpu as pltpu
from jax.sharding import PartitionSpec as P

BINS = 256
LANES = 128
HIGH = 4
LOW = BINS // HIGH
NODE_ROWS = 2 * HIGH

shrinkage = 1.0


def histogram_kernel(bin_ref, node_ref, grad_ref, hess_ref, table_ref, row_key, low_key, weight):
    feature_count, row_count = bin_ref.shape
    node_count, pair_count = table_ref.shape[:2]
    product_rows = node_count * NODE_ROWS

    bins = bin_ref[...]
    row_key[...] = node_ref[...] * HIGH + bins // LOW
    low_key[...] = bins & (LOW - 1)
    slot = lax.broadcasted_iota(jnp.int32, (2 * NODE_ROWS, row_count), 0)
    is_grad = (slot & HIGH) == 0
    value = jnp.where(is_grad, grad_ref[...], hess_ref[...])
    weight[...] = value.astype(jnp.float32).astype(jnp.bfloat16)

    slot = lax.broadcasted_iota(jnp.int32, (product_rows, row_count), 0)
    wanted_row = ((slot // NODE_ROWS) * HIGH + (slot & (HIGH - 1))).astype(jnp.int16)
    wanted_low = lax.broadcasted_iota(jnp.int32, (LOW, row_count), 0).astype(jnp.int16)
    zero = jnp.zeros((), jnp.bfloat16)
    one = jnp.ones((), jnp.bfloat16)
    first_half = lax.broadcasted_iota(jnp.int32, (product_rows, LANES), 1) < LOW

    def one_hots(feature):
        key = jnp.broadcast_to(row_key[pl.ds(feature, 1), :], (product_rows, row_count))
        low = jnp.broadcast_to(low_key[pl.ds(feature, 1), :], (LOW, row_count))
        values = jnp.concatenate([weight[...]] * (product_rows // (2 * NODE_ROWS)), axis=0)
        left = jnp.where(key.astype(jnp.int16) == wanted_row, values, zero)
        right = jnp.where(low.astype(jnp.int16) == wanted_low, one, zero)
        return left, right

    @pl.loop(0, pair_count, unroll=2)
    def _(pair):
        left_a, right_a = one_hots(pair)
        left_b, right_b = one_hots(pair + pair_count)
        both = lax.dot_general(
            jnp.concatenate([left_a, left_b], axis=0),
            jnp.concatenate([right_a, right_b], axis=0),
            (((1,), (1,)), ((), ())),
            preferred_element_type=jnp.float32,
        )
        own = jnp.where(first_half, both[:product_rows], both[product_rows:])
        table_ref[:, pair] = own.reshape(node_count, NODE_ROWS, LANES)


def histograms(bin_index, node_ids, gradients, hessians, node_count):
    feature_count, row_count = bin_index.shape
    return pl.pallas_call(
        histogram_kernel,
        out_shape=jax.ShapeDtypeStruct(
            (node_count, feature_count // 2, NODE_ROWS, LANES), jnp.float32
        ),
        scratch_shapes=[
            pltpu.VMEM((feature_count, row_count), jnp.int32),
            pltpu.VMEM((feature_count, row_count), jnp.int32),
            pltpu.VMEM((2 * NODE_ROWS, row_count), jnp.bfloat16),
        ],
        name="histograms",
    )(
        bin_index,
        node_ids.reshape(1, row_count),
        gradients.reshape(1, row_count),
        hessians.reshape(1, row_count),
    )


def prefix_sums(first, second):
    lane = lax.broadcasted_iota(jnp.int32, first.shape, 1)
    step = 1
    while step < LANES:
        first = first + jnp.where(lane >= step, pltpu.roll(first, step, axis=1), 0.0)
        second = second + jnp.where(lane >= step, pltpu.roll(second, step, axis=1), 0.0)
        step *= 2
    return first, second + first[:, LANES - 1 :]


def gains_kernel(parts_ref, gains_ref, best_ref, table):
    pair_count = parts_ref.shape[1]
    table[...] = jnp.sum(parts_ref[...], axis=0).reshape(pair_count * NODE_ROWS, LANES)
    lane = lax.broadcasted_iota(jnp.int32, (pair_count, LANES), 1)
    sums = []
    for value in range(2):
        rows = [
            table[pl.ds(value * HIGH + high, pair_count, stride=NODE_ROWS), :]
            for high in range(HIGH)
        ]
        turned = [pltpu.roll(row, LOW, axis=1) for row in rows]
        halves = []
        for half in range(2):
            tiles = []
            for at in range(0, HIGH, 2):
                left = rows[at] if half == 0 else turned[at]
                right = turned[at + 1] if half == 0 else rows[at + 1]
                tiles.append(jnp.where(lane < LOW, left, right))
            halves.append(prefix_sums(*tiles))
        sums.append(halves)
    best = None
    for half in range(2):
        grad, hess = sums[0][half], sums[1][half]
        total_grad = grad[1][:, LANES - 1 :]
        total_hess = hess[1][:, LANES - 1 :]
        whole = total_grad * total_grad / (total_hess + shrinkage)
        for at in range(2):
            left_grad, left_hess = grad[at], hess[at]
            right_grad = total_grad - left_grad
            right_hess = total_hess - left_hess
            gains = 0.5 * (
                left_grad * left_grad / (left_hess + shrinkage)
                + right_grad * right_grad / (right_hess + shrinkage)
                - whole
            )
            gains_ref[0, pl.ds(half * pair_count, pair_count), pl.ds(at * LANES, LANES)] = gains
            best = gains if best is None else jnp.maximum(best, gains)
    best_ref[0] = jnp.max(best)


def split_gains_of(parts):
    pair_count = parts.shape[1]
    return pl.pallas_call(
        gains_kernel,
        out_shape=(
            jax.ShapeDtypeStruct((1, 2 * pair_count, BINS), jnp.float32),
            jax.ShapeDtypeStruct((1,), jnp.float32),
        ),
        out_specs=(
            pl.BlockSpec(memory_space=pltpu.VMEM),
            pl.BlockSpec(memory_space=pltpu.SMEM),
        ),
        scratch_shapes=[pltpu.VMEM((pair_count * NODE_ROWS, LANES), jnp.float32)],
        name="gains",
    )(parts)


def per_device(bin_index, node_ids, gradients, hessians):
    node_count = lax.axis_size("rows")
    table = histograms(bin_index, node_ids, gradients, hessians, node_count)
    parts = lax.all_to_all(table, "rows", 0, 0, tiled=True)
    split_gains, local_best = split_gains_of(parts)
    best_gains = lax.pmax(local_best, "feat")
    return split_gains, best_gains


def solution(mesh):
    in_specs = (P("feat", "rows"), P("rows"), P("rows"), P("rows"))
    out_specs = (P("rows", "feat", None), P("rows"))
    return jax.shard_map(
        per_device, mesh=mesh, in_specs=in_specs, out_specs=out_specs, check_vma=False
    )
```

time: 125 us -> 33.1 us (0.26)
  waiting for transfers between devices: 65.3 us -> 0 us
  matrix products: 25.6 us -> 0 us
  blocking collectives: 6.27 us -> 22.6 us
  between operations: 14.3 us -> 0.64 us
  Pallas kernels: 0 us -> 9.54 us
  local copies, waits for them, and re-layouts: 8.03 us -> 0 us
  other arithmetic: 3.53 us -> 0 us
  loops' own time: 1.41 us -> 0 us
    reduce_scatter x1 -> x0, waiting for transfers between devices: 65.3 us -> none  [per_device(): lax.psum_scatter(whole_table, 'rows', scatter_dimension=0, tiled=True)]
    dot_general x32 -> x0, matrix products: 25.6 us -> none  [accumulate(): lax.dot_general(weighted, bin_hot, (((0,), (0,)), ((), ())), preferred_el...]
    all_to_all x0 -> x1, blocking collectives: none -> 16.3 us  [per_device(): parts = lax.all_to_all(table, 'rows', 0, 0, tiled=True)]
    pallas_call x0 -> x2, Pallas kernels: none -> 9.54 us  [the longest x1 7.24 us: histograms(): pl.pallas_call(histogram_kernel, out_shape=jax.ShapeDtypeStruct((node_cou...]
    dynamic_slice x6 -> x0, local copies, waits for them, and re-layouts: 2.63 us -> none  [the longest x2 1.45 us: accumulate(): nodes_here = lax.dynamic_slice_in_dim(node_ids, offset, row_block, 0)]
    another operation x28 -> x0, local copies, waits for them, and re-layouts: 2.55 us -> none  [the longest x17 2.02 us: per_device(): joined = jnp.stack(summed, axis=1)]
    slice x4 -> x0, local copies, waits for them, and re-layouts: 2.11 us -> none  [the longest x2 1.21 us: accumulate(): bins_here[feature_index][:, None] == bin_values[None, :]]
    another operation x1 -> x0, loops' own time: 1.41 us -> none  [per_device(): lax.scan(accumulate, start_sums, jnp.arange(block_count, dtype=jnp.int32))]
  transfers between devices with their start and end apart: 1 -> 0, of which waited for: 1 -> 0; matrix products, arithmetic and copies ran while one was open for 0% -> 0% of each run, Pallas kernels for 0% -> 0%
where the time goes in v1:
time: 33.1 us; the launch traced here: 32.8 us
  blocking collectives  22.6 us (68%)
  Pallas kernels  9.54 us (29%)
  between operations  0.64 us (2%)
    all_to_all x1, blocking collectives, per_device(): parts = lax.all_to_all(table, 'rows', 0, 0, tiled=True)  16.3 us
    pallas_call x1, Pallas kernels, histograms(): pl.pallas_call(histogram_kernel, out_shape=jax.ShapeDtypeStruct((node_cou...  7.24 us
    pmax x1, blocking collectives, per_device(): best_gains = lax.pmax(local_best, 'feat')  6.3 us
    pallas_call x1, Pallas kernels, split_gains_of(): pl.pallas_call(gains_kernel, out_shape=(jax.ShapeDtypeStruct((1, 2 * pair...  2.3 us

profile of v1, /device:TPU:0, one launch (start us, length us, event | category | flops | bytes accessed | tf_op | source)
XLA Modules:
  0.0 32.8 jit_solution(1847106173733445725)
XLA Ops:
  0.6 7.2 %histograms.1 = f32[8,8,8,128]{3,2,1,0:T(8,128)} custom-call(s32[16,8192]{1,0:T(8,128)} %bin_ref.1, s32[1,8192]{1,0:T(1,128)} %bitcast.3, s32[1,8192]{1,0:T(1,128)} %bitcast.4, s32[1,8192]{1,0:T(1,128)} %bitcast.5), custom_call_target="tpu_custom_call" | custom-call | tf_op jit(solution)/shard_map/histograms/pallas_call | solution.py:63
  7.9 16.3 %all_to_all.5.parts_ref = f32[8,8,8,128]{3,2,1,0:T(8,128)} all-to-all(f32[8,8,8,128]{3,2,1,0:T(8,128)} %histograms.1), channel_id=1, replica_groups=mesh['feat'=4,'rows'=8] {'rows'}, dimensions={0} | all-to-all | bytes 524288 | tf_op jit(solution)/shard_map/all_to_all | solution.py:152
  24.2 2.3 %gains.1 = (f32[1,16,256]{2,1,0:T(8,128)}, f32[1]{0:T(128)}) custom-call(f32[8,8,8,128]{3,2,1,0:T(8,128)} %all_to_all.5.parts_ref), custom_call_target="tpu_custom_call" | custom-call | tf_op jit(solution)/shard_map/gains/pallas_call | solution.py:134
  26.5 6.3 %pmax.7 = f32[1]{0:T(128)} all-reduce(f32[1]{0:T(128)} %get-tuple-element.5), channel_id=1, replica_groups=mesh['feat'=4,'rows'=8] {'feat'}, use_global_device_ids=true, to_apply=%region_0.0 | all-reduce | flops 1 | bytes 8 | tf_op jit(solution)/shard_map/pmax | solution.py:154
